TPU v7x, 256 devices: a whole 4x4x8 slice. The times are simulated.
256 devices in a mesh: gx: 8 (over x, core), gy: 4 (over z_lo), gz: 8 (over y, z_hi).
Axes of the slice: x: 4, y: 4, z: 8 (z_hi: 2, z_lo: 4; z = z_hi * 4 + z_lo), core: 2. Of those that a mesh axis runs over, the one named last changes fastest.
Arguments:
- start_block: float32 [32, 3, 2, 8, 16, 1024], P(None, None, None, 'gx', 'gy', 'gz'), may hold values from -700 to 700
- pair_blocks: float32 [3, 3, 16, 2, 8, 16, 1024], P(None, None, None, None, 'gx', 'gy', 'gz'), may hold values from -8 to 8, as said below
- slot_map: int32 [16, 2, 8, 16, 1024], P(None, None, 'gx', 'gy', 'gz'), may hold values from 0 to 15, as said below
Outputs:
- alpha1: float32 [32, 32], replicated
- alpha2: float32 [32, 32], replicated
- beta1: float32 [32, 32], replicated
- beta2: float32 [32, 32], replicated
- basis3: float32 [32, 3, 2, 8, 16, 1024], P(None, None, None, 'gx', 'gy', 'gz')
Inputs may be any that keep to these rules, and one draw needn't show every extreme that they name: `slot_map`: for every atom the 16 slots hold each of 0 to 15 once; 0 to 13 name the neighbour directions of the steps, 14 and 15 mark padding slots. `pair_blocks`: the block an atom holds toward a neighbour is the transpose of the block that neighbour holds toward the atom, so H is symmetric.
All inputs are finite; a program needn't handle non-finite values.
Results may differ from a plain program's by a relative error of at most 0.0003.
Values sent between devices are 32-bit elements; how exact they have to be, the bound alone decides.
A program may use at most 64 MiB of HBM per device.

v0:
```python
import jax
import jax.numpy as jnp
from jax import lax
from jax.sharding import PartitionSpec as P

PRECISE = lax.Precision.HIGHEST


def extended(block, sides, width):
    for axis, dim in sides:
        count = lax.axis_size(axis)
        forward = [(i, i + 1) for i in range(count - 1)]
        forward.append((count - 1, 0))
        backward = [(target, source) for source, target in forward]
        low = lax.ppermute(
            lax.slice_in_dim(block, block.shape[dim] - width, None, axis=dim), axis, forward
        )
        high = lax.ppermute(lax.slice_in_dim(block, 0, width, axis=dim), axis, backward)
        block = jnp.concatenate([low, block, high], axis=dim)
    return block


def neighbour_offset(sublattice, offset_id):
    if offset_id < 8:
        corner_bits = (offset_id >> 2 & 1, offset_id >> 1 & 1, offset_id & 1)
        if sublattice == 0:
            return ((-corner_bits[0], -corner_bits[1], -corner_bits[2]), 1)
        return (corner_bits, 0)
    axis_id = (offset_id - 8) // 2
    direction = 1 if (offset_id - 8) % 2 == 0 else -1
    displacement = tuple((direction if axis_number == axis_id else 0 for axis_number in range(3)))
    return (displacement, sublattice)


def offset_blocks(pair_blocks, slot_map):
    result = []
    for offset_id in range(14):
        chosen = slot_map[None, None] == offset_id
        result.append(jnp.sum(jnp.where(chosen, pair_blocks, jnp.float32(0.0)), axis=2))
    return result


def onsite_blocks(blocks):
    result = []
    for sublattice in range(2):
        onsite = jnp.zeros(blocks[0].shape[:2] + blocks[0].shape[3:], jnp.float32)
        for offset_id in range(14):
            coupling = blocks[offset_id][:, :, sublattice]
            onsite = onsite + 0.5 * (coupling + jnp.swapaxes(coupling, 0, 1))
        result.append(onsite)
    return result


def apply_hessian(vectors, blocks, onsite):
    padded = extended(vectors, (("gx", 3), ("gy", 4), ("gz", 5)), 1)
    size_x, size_y, size_z = (vectors.shape[3], vectors.shape[4], vectors.shape[5])
    outputs = []
    for sublattice in range(2):
        summed = jnp.zeros(vectors.shape[:2] + vectors.shape[3:], jnp.float32)
        for offset_id in range(14):
            displacement, source = neighbour_offset(sublattice, offset_id)
            start_x = 1 + displacement[0]
            start_y = 1 + displacement[1]
            start_z = 1 + displacement[2]
            neighbour = padded[
                :,
                :,
                source,
                start_x : start_x + size_x,
                start_y : start_y + size_y,
                start_z : start_z + size_z,
            ]
            coupling = blocks[offset_id][:, :, sublattice]
            summed = summed + jnp.sum(coupling[None] * neighbour[:, None], axis=2)
        summed = summed - jnp.sum(
            onsite[sublattice][None] * vectors[:, None, :, sublattice], axis=2
        )
        outputs.append(summed)
    return jnp.stack(outputs, axis=2)


def local_gram(left, right):
    left_flat = left.reshape(left.shape[0], -1)
    right_flat = right.reshape(right.shape[0], -1)
    return lax.dot_general(left_flat, right_flat, (((1,), (1,)), ((), ())), precision=PRECISE)


def combine(matrix, vectors):
    flat = vectors.reshape(vectors.shape[0], -1)
    return jnp.dot(matrix, flat, precision=PRECISE).reshape(vectors.shape)


def inverse_factor(gram_matrix):
    lower = jnp.linalg.cholesky(gram_matrix)
    identity = jnp.eye(gram_matrix.shape[0], dtype=gram_matrix.dtype)
    inverse = jax.scipy.linalg.solve_triangular(lower, identity, lower=True)
    return (lower, inverse)


def lanczos_step(basis, image, previous, coupling_prev, row_count):
    alpha = lax.psum(local_gram(image, basis), ("gx", "gy", "gz")) / row_count
    residual = image - combine(alpha, basis)
    if previous is not None:
        residual = residual - combine(coupling_prev.T, previous)
    residual_gram = lax.psum(local_gram(residual, residual), ("gx", "gy", "gz")) / row_count
    return (alpha, residual, residual_gram)


def local(start_block, pair_blocks, slot_map):
    device_count = lax.axis_size("gx") * lax.axis_size("gy") * lax.axis_size("gz")
    row_count = start_block[0].size * device_count
    blocks = offset_blocks(pair_blocks, slot_map)
    onsite = onsite_blocks(blocks)
    start_gram = lax.psum(local_gram(start_block, start_block), ("gx", "gy", "gz")) / row_count
    lower0, inverse0 = inverse_factor(start_gram)
    basis1 = combine(inverse0, start_block)
    image1 = apply_hessian(basis1, blocks, onsite)
    alpha1, residual1, gram_first = lanczos_step(basis1, image1, None, None, row_count)
    beta1, inverse1 = inverse_factor(gram_first)
    basis2 = combine(inverse1, residual1)
    image2 = apply_hessian(basis2, blocks, onsite)
    alpha2, residual2, gram_second = lanczos_step(basis2, image2, basis1, beta1, row_count)
    beta2, inverse2 = inverse_factor(gram_second)
    basis3 = combine(inverse2, residual2)
    return (alpha1, alpha2, beta1, beta2, basis3)


def solution(mesh):
    in_specs = (
        P(None, None, None, "gx", "gy", "gz"),
        P(None, None, None, None, "gx", "gy", "gz"),
        P(None, None, "gx", "gy", "gz"),
    )
    out_specs = (P(), P(), P(), P(), P(None, None, None, "gx", "gy", "gz"))
    return jax.shard_map(local, mesh=mesh, in_specs=in_specs, out_specs=out_specs, check_vma=False)
```

profile of v0, /device:TPU:1, one launch (start us, length us, event | category | flops | bytes accessed | tf_op | source)
XLA Modules:
  0.0 522.5 jit_solution(3226206658296597986)
XLA Ops:
  0.6 1.2 reshape.1549
  1.8 1.6 convolution_bitcast_fusion.2
  3.4 81.5 %psum.35 = f32[32,32]{0,1:T(8,128)S(1)} all-reduce(f32[32,32]{0,1:T(8,128)S(1)} %convolution_bitcast_fusion.2), channel_id=1, replica_groups=mesh['gx'=8,'gy'=4,'gz'=8] {'gx','gy','gz'}, use_global_device_ids=true, to_apply=%region_1.2 | all-reduce | flops 1024 | bytes 8192 | tf_op jit(solution)/shard_map/psum | solution.py:114
  85.0 2.9 cholesky.59
  89.3 2.4 custom-call.7
  92.8 1.0 collective-permute-start.1
  94.1 2.5 select_reduce_fusion.13
  106.4 2.7 collective-permute-start.3
  111.5 0.9 multiply_reduce_fusion.51
  112.3 1.1 collective-permute-done.2
  113.4 6.9 %collective-permute-done.3 = f32[32,3,2,3,1,128]{5,0,4,3,2,1:T(8,128)S(1)} collective-permute-done((f32[32,3,2,3,1,128]{5,0,4,3,2,1:T(8,128)S(1)}, f32[32,3,2,3,1,128]{5,0,4,3,2,1:T(8,128)S(1)}, u32[]{:S(2)}, u32[]{:S(2)}) %collective-permute-start.3) | collective-permute-done | bytes 294944 | tf_op jit(solution)/shard_map/ppermute | solution.py:18
  121.2 1.8 fusion.52
  123.1 2.8 copy.507
  125.9 5.6 %collective-permute-start.5 = (f32[32,3,2,3,6,1]{0,2,5,4,3,1:T(2,128)}, f32[32,3,2,3,6,1]{0,2,5,4,3,1:T(2,128)}, u32[]{:S(2)}, u32[]{:S(2)}) collective-permute-start(f32[32,3,2,3,6,1]{0,2,5,4,3,1:T(2,128)} %copy.507), channel_id=1, source_target_pairs={{1,0},{2,1},{3,2},{4,3},{5,4},{6,5},{7,6},{0,7},{9,8},{10,9},{11,1... | collective-permute-start | bytes 41480 | tf_op jit(solution)/shard_map/ppermute | solution.py:18
  131.5 1.3 copy.506
  132.8 1.7 multiply_reduce_fusion.36
  134.5 2.7 copy.419
  137.2 5.0 collective-permute-done.4
  142.2 1.5 copy.395
  143.8 1.4 fusion.8
  151.0 74.3 %psum.36 = f32[32,32]{0,1:T(8,128)S(1)} all-reduce(f32[32,32]{0,1:T(8,128)S(1)} %fusion.56), channel_id=1, replica_groups=mesh['gx'=8,'gy'=4,'gz'=8] {'gx','gy','gz'}, use_global_device_ids=true, to_apply=%region_47.50 | all-reduce | flops 1024 | bytes 8192 | tf_op jit(solution)/shard_map/psum | solution.py:101
  226.4 73.7 %psum.37 = f32[32,32]{0,1:T(8,128)S(1)} all-reduce(f32[32,32]{0,1:T(8,128)S(1)} %fusion.57), channel_id=1, replica_groups=mesh['gx'=8,'gy'=4,'gz'=8] {'gx','gy','gz'}, use_global_device_ids=true, to_apply=%region_48.51 | all-reduce | flops 1024 | bytes 8192 | tf_op jit(solution)/shard_map/psum | solution.py:105
  300.2 2.9 cholesky.70
  304.4 2.4 custom-call.8
  307.9 1.2 collective-permute-start.6
  311.7 2.2 collective-permute-done.6
  314.0 2.6 collective-permute-done.7
  316.7 1.0 collective-permute-start.8
  317.7 2.4 collective-permute-start.9
  322.6 4.1 collective-permute-done.8
  326.7 5.3 %collective-permute-done.9 = f32[32,3,2,3,1,128]{5,0,4,3,2,1:T(8,128)S(1)} collective-permute-done((f32[32,3,2,3,1,128]{5,0,4,3,2,1:T(8,128)S(1)}, f32[32,3,2,3,1,128]{5,0,4,3,2,1:T(8,128)S(1)}, u32[]{:S(2)}, u32[]{:S(2)}) %collective-permute-start.9) | collective-permute-done | bytes 294944 | tf_op jit(solution)/shard_map/ppermute | solution.py:18
  332.9 1.8 fusion.51
  334.8 2.8 copy.509
  337.6 4.7 collective-permute-start.11
  342.2 1.5 multiply_reduce_fusion.6
  343.7 1.3 copy.508
  345.7 1.5 copy.488
  347.2 2.2 maximum_bitcast_fusion.4
  349.5 0.9 multiply_reduce_fusion.17
  350.4 4.6 collective-permute-done.10
  354.9 1.5 copy.486
  356.5 1.4 fusion.4
  363.7 73.7 %psum.38 = f32[32,32]{0,1:T(8,128)S(1)} all-reduce(f32[32,32]{0,1:T(8,128)S(1)} %fusion.59), channel_id=1, replica_groups=mesh['gx'=8,'gy'=4,'gz'=8] {'gx','gy','gz'}, use_global_device_ids=true, to_apply=%region_79.82 | all-reduce | flops 1024 | bytes 8192 | tf_op jit(solution)/shard_map/psum | solution.py:101
  439.1 73.7 %psum.39 = f32[32,32]{0,1:T(8,128)S(1)} all-reduce(f32[32,32]{0,1:T(8,128)S(1)} %fusion.60), channel_id=1, replica_groups=mesh['gx'=8,'gy'=4,'gz'=8] {'gx','gy','gz'}, use_global_device_ids=true, to_apply=%region_80.83 | all-reduce | flops 1024 | bytes 8192 | tf_op jit(solution)/shard_map/psum | solution.py:105
  512.8 2.9 cholesky.81
  516.4 1.3 select_bitcast_fusion
  517.6 2.4 custom-call.9
  520.8 1.0 copy.497
  (337 shorter events, 40.4 us)
Async XLA Ops:
  3.4 90.4 %copy-start.95 = (s32[16,2,1,4,128]{4,3,2,1,0:T(4,128)S(1)}, s32[16,2,1,4,128]{4,3,2,1,0:T(4,128)}, u32[]{:S(2)}) copy-start(s32[16,2,1,4,128]{4,3,2,1,0:T(4,128)} %param.8) | copy-start | bytes 196612
  88.6 5.5 %copy-start.35 = (f32[3,3,16,2,1,4,128]{6,5,4,3,2,1,0:T(4,128)S(1)}, f32[3,3,16,2,1,4,128]{6,5,4,3,2,1,0:T(4,128)}, u32[]{:S(2)}) copy-start(f32[3,3,16,2,1,4,128]{6,5,4,3,2,1,0:T(4,128)} %param.7) | copy-start | bytes 1769476
  92.8 12.8 %collective-permute-start = (f32[32,3,2,1,4,128]{5,0,4,3,2,1:T(8,128)S(1)}, f32[32,3,2,1,4,128]{5,0,4,3,2,1:T(8,128)S(1)}, u32[]{:S(2)}, u32[]{:S(2)}) collective-permute-start(f32[32,3,2,1,4,128]{5,0,4,3,2,1:T(8,128)S(1)} %copy.391), channel_id=1, source_target_pairs={{0,32},{32,64},{64,96},{96,128},{128,160},{160,192},{192,224},{224... | collective-permute-start | bytes 1179656 | tf_op jit(solution)/shard_map/ppermute | solution.py:15
  92.8 12.9 %collective-permute-start.1 = (f32[32,3,2,1,4,128]{5,0,4,3,2,1:T(8,128)S(1)}, f32[32,3,2,1,4,128]{5,0,4,3,2,1:T(8,128)S(1)}, u32[]{:S(2)}, u32[]{:S(2)}) collective-permute-start(f32[32,3,2,1,4,128]{5,0,4,3,2,1:T(8,128)S(1)} %copy.391), channel_id=1, source_target_pairs={{32,0},{64,32},{96,64},{128,96},{160,128},{192,160},{224,192},{0,2... | collective-permute-start | bytes 1179656 | tf_op jit(solution)/shard_map/ppermute | solution.py:18
  99.9 10.0 %copy-start.84 = (f32[3,3,4,128]{3,2,0,1:T(4,128)}, f32[3,3,4,128]{3,2,0,1:T(4,128)S(1)}, u32[]{:S(2)}) copy-start(f32[3,3,4,128]{3,2,0,1:T(4,128)S(1)} %get-tuple-element.159) | copy-start | bytes 55300
  99.9 10.7 %copy-start.82 = (f32[3,3,4,128]{3,2,0,1:T(4,128)}, f32[3,3,4,128]{3,2,0,1:T(4,128)S(1)}, u32[]{:S(2)}) copy-start(f32[3,3,4,128]{3,2,0,1:T(4,128)S(1)} %get-tuple-element.162) | copy-start | bytes 55300
  100.5 10.9 %copy-start.80 = (f32[3,3,4,128]{3,2,0,1:T(4,128)}, f32[3,3,4,128]{3,2,0,1:T(4,128)S(1)}, u32[]{:S(2)}) copy-start(f32[3,3,4,128]{3,2,0,1:T(4,128)S(1)} %get-tuple-element.194) | copy-start | bytes 55300
  102.5 8.1 %copy-start.88 = (f32[3,3,4,128]{3,2,0,1:T(4,128)}, f32[3,3,4,128]{3,2,0,1:T(4,128)S(1)}, u32[]{:S(2)}) copy-start(f32[3,3,4,128]{3,2,0,1:T(4,128)S(1)} %get-tuple-element.190) | copy-start | bytes 55300
  102.5 9.0 %copy-start.86 = (f32[3,3,4,128]{3,2,0,1:T(4,128)}, f32[3,3,4,128]{3,2,0,1:T(4,128)S(1)}, u32[]{:S(2)}) copy-start(f32[3,3,4,128]{3,2,0,1:T(4,128)S(1)} %get-tuple-element.189) | copy-start | bytes 55300
  103.8 1.8 copy-start.90
  103.8 1.8 copy-start.92
  103.9 1.9 copy-start.36
  105.8 7.6 %collective-permute-start.2 = (f32[32,3,2,3,1,128]{5,0,4,3,2,1:T(8,128)S(1)}, f32[32,3,2,3,1,128]{5,0,4,3,2,1:T(8,128)S(1)}, u32[]{:S(2)}, u32[]{:S(2)}) collective-permute-start(f32[32,3,2,3,1,128]{5,0,4,3,2,1:T(8,128)S(1)} %get-tuple-element.115), channel_id=1, source_target_pairs={{0,8},{8,16},{16,24},{24,0},{1,9},{9,17},{17,25},{25,1},{2,10},{10... | collective-permute-start | bytes 884744 | tf_op jit(solution)/shard_map/ppermute | solution.py:15
  106.4 13.9 %collective-permute-start.3 = (f32[32,3,2,3,1,128]{5,0,4,3,2,1:T(8,128)S(1)}, f32[32,3,2,3,1,128]{5,0,4,3,2,1:T(8,128)S(1)}, u32[]{:S(2)}, u32[]{:S(2)}) collective-permute-start(f32[32,3,2,3,1,128]{5,0,4,3,2,1:T(8,128)S(1)} %get-tuple-element.116), channel_id=1, source_target_pairs={{8,0},{16,8},{24,16},{0,24},{9,1},{17,9},{25,17},{1,25},{10,2},{18... | collective-permute-start | bytes 884744 | tf_op jit(solution)/shard_map/ppermute | solution.py:18
  113.4 6.9 %copy-start.8 = (f32[32,3,2,3,1,128]{5,0,4,3,2,1:T(8,128)}, f32[32,3,2,3,1,128]{5,0,4,3,2,1:T(8,128)S(1)}, u32[]{:S(2)}) copy-start(f32[32,3,2,3,1,128]{5,0,4,3,2,1:T(8,128)S(1)} %collective-permute-done.2) | copy-start | bytes 884740
  125.9 8.6 %collective-permute-start.5 = (f32[32,3,2,3,6,1]{0,2,5,4,3,1:T(2,128)}, f32[32,3,2,3,6,1]{0,2,5,4,3,1:T(2,128)}, u32[]{:S(2)}, u32[]{:S(2)}) collective-permute-start(f32[32,3,2,3,6,1]{0,2,5,4,3,1:T(2,128)} %copy.507), channel_id=1, source_target_pairs={{1,0},{2,1},{3,2},{4,3},{5,4},{6,5},{7,6},{0,7},{9,8},{10,9},{11,1... | collective-permute-start | bytes 41480 | tf_op jit(solution)/shard_map/ppermute | solution.py:18
  132.8 9.4 %collective-permute-start.4 = (f32[32,3,2,3,6,1]{0,2,5,4,3,1:T(2,128)}, f32[32,3,2,3,6,1]{0,2,5,4,3,1:T(2,128)}, u32[]{:S(2)}, u32[]{:S(2)}) collective-permute-start(f32[32,3,2,3,6,1]{0,2,5,4,3,1:T(2,128)} %copy.506), channel_id=1, source_target_pairs={{0,1},{1,2},{2,3},{3,4},{4,5},{5,6},{6,7},{7,0},{8,9},{9,10},{10,1... | collective-permute-start | bytes 41480 | tf_op jit(solution)/shard_map/ppermute | solution.py:15
  143.8 1.5 copy-start.72
  143.8 1.5 copy-start.9
  143.8 1.5 copy-start.11
  145.4 1.5 copy-start
  304.4 133.4 %copy-start.94 = (f32[32,32]{1,0:T(8,128)}, f32[32,32]{1,0:T(8,128)S(1)}, u32[]{:S(2)}) copy-start(f32[32,32]{1,0:T(8,128)S(1)} %get-tuple-element.76) | copy-start | bytes 12292
  307.1 2.1 copy-start.37
  307.1 2.1 copy-start.93
  307.6 2.5 copy-start.2
  307.6 2.5 copy-start.39
  307.6 2.5 copy-start.91
  307.9 5.9 %collective-permute-start.6 = (f32[32,3,2,1,4,128]{5,0,4,3,2,1:T(8,128)S(1)}, f32[32,3,2,1,4,128]{5,0,4,3,2,1:T(8,128)S(1)}, u32[]{:S(2)}, u32[]{:S(2)}) collective-permute-start(f32[32,3,2,1,4,128]{5,0,4,3,2,1:T(8,128)S(1)} %copy.482), channel_id=1, source_target_pairs={{0,32},{32,64},{64,96},{96,128},{128,160},{160,192},{192,224},{224... | collective-permute-start | bytes 1179656 | tf_op jit(solution)/shard_map/ppermute | solution.py:15
  309.1 7.5 %collective-permute-start.7 = (f32[32,3,2,1,4,128]{5,0,4,3,2,1:T(8,128)S(1)}, f32[32,3,2,1,4,128]{5,0,4,3,2,1:T(8,128)S(1)}, u32[]{:S(2)}, u32[]{:S(2)}) collective-permute-start(f32[32,3,2,1,4,128]{5,0,4,3,2,1:T(8,128)S(1)} %copy.482), channel_id=1, source_target_pairs={{32,0},{64,32},{96,64},{128,96},{160,128},{192,160},{224,192},{0,2... | collective-permute-start | bytes 1179656 | tf_op jit(solution)/shard_map/ppermute | solution.py:18
  314.0 6.2 %copy-start.85 = (f32[3,3,4,128]{3,2,0,1:T(4,128)S(1)}, f32[3,3,4,128]{3,2,0,1:T(4,128)}, u32[]{:S(2)}) copy-start(f32[3,3,4,128]{3,2,0,1:T(4,128)} %copy-done.84) | copy-start | bytes 55300
  316.7 4.2 copy-start.83
  316.7 4.2 copy-start.89
  316.7 5.1 copy-start.81
  316.7 5.1 copy-start.87
  316.7 10.0 %collective-permute-start.8 = (f32[32,3,2,3,1,128]{5,0,4,3,2,1:T(8,128)S(1)}, f32[32,3,2,3,1,128]{5,0,4,3,2,1:T(8,128)S(1)}, u32[]{:S(2)}, u32[]{:S(2)}) collective-permute-start(f32[32,3,2,3,1,128]{5,0,4,3,2,1:T(8,128)S(1)} %get-tuple-element.113), channel_id=1, source_target_pairs={{0,8},{8,16},{16,24},{24,0},{1,9},{9,17},{17,25},{25,1},{2,10},{10... | collective-permute-start | bytes 884744 | tf_op jit(solution)/shard_map/ppermute | solution.py:15
  317.7 14.3 %collective-permute-start.9 = (f32[32,3,2,3,1,128]{5,0,4,3,2,1:T(8,128)S(1)}, f32[32,3,2,3,1,128]{5,0,4,3,2,1:T(8,128)S(1)}, u32[]{:S(2)}, u32[]{:S(2)}) collective-permute-start(f32[32,3,2,3,1,128]{5,0,4,3,2,1:T(8,128)S(1)} %get-tuple-element.114), channel_id=1, source_target_pairs={{8,0},{16,8},{24,16},{0,24},{9,1},{17,9},{25,17},{1,25},{10,2},{18... | collective-permute-start | bytes 884744 | tf_op jit(solution)/shard_map/ppermute | solution.py:18
  326.7 5.3 %copy-start.4 = (f32[32,3,2,3,1,128]{5,0,4,3,2,1:T(8,128)}, f32[32,3,2,3,1,128]{5,0,4,3,2,1:T(8,128)S(1)}, u32[]{:S(2)}) copy-start(f32[32,3,2,3,1,128]{5,0,4,3,2,1:T(8,128)S(1)} %collective-permute-done.8) | copy-start | bytes 884740
  337.6 8.1 %collective-permute-start.11 = (f32[32,3,2,3,6,1]{0,2,5,4,3,1:T(2,128)}, f32[32,3,2,3,6,1]{0,2,5,4,3,1:T(2,128)}, u32[]{:S(2)}, u32[]{:S(2)}) collective-permute-start(f32[32,3,2,3,6,1]{0,2,5,4,3,1:T(2,128)} %copy.509), channel_id=1, source_target_pairs={{1,0},{2,1},{3,2},{4,3},{5,4},{6,5},{7,6},{0,7},{9,8},{10,9},{11,1... | collective-permute-start | bytes 41480 | tf_op jit(solution)/shard_map/ppermute | solution.py:18
  345.0 9.9 %collective-permute-start.10 = (f32[32,3,2,3,6,1]{0,2,5,4,3,1:T(2,128)}, f32[32,3,2,3,6,1]{0,2,5,4,3,1:T(2,128)}, u32[]{:S(2)}, u32[]{:S(2)}) collective-permute-start(f32[32,3,2,3,6,1]{0,2,5,4,3,1:T(2,128)} %copy.508), channel_id=1, source_target_pairs={{0,1},{1,2},{2,3},{3,4},{4,5},{5,6},{6,7},{7,0},{8,9},{9,10},{10,1... | collective-permute-start | bytes 41480 | tf_op jit(solution)/shard_map/ppermute | solution.py:15
  347.2 2.2 copy-start.1
  347.2 2.2 copy-start.59
  347.2 2.2 copy-start.63
  356.4 1.4 copy-start.65
  356.5 1.5 copy-start.79
  356.5 1.6 copy-start.55
  356.5 1.6 copy-start.73
  356.5 1.7 copy-start.57
  356.5 1.7 copy-start.77
  (60 other events, 58.4 us)
where the time goes:
time: 524 us; the launch traced here: 522 us
  blocking collectives  377 us (72%)
  other arithmetic  45.5 us (9%)
  local copies, waits for them, and re-layouts  39 us (7%)
  waiting for transfers between devices  31.8 us (6%)
  starting transfers between devices  19.9 us (4%)
  matrix products  7.11 us (1%)
    psum x2, blocking collectives, lanczos_step(): alpha = lax.psum(local_gram(image, basis), ('gx', 'gy', 'gz')) / row_count  148 us
    psum x2, blocking collectives, lanczos_step(): lax.psum(local_gram(residual, residual), ('gx', 'gy', 'gz')) / row_count  147 us
    psum x1, blocking collectives, local(): lax.psum(local_gram(start_block, start_block), ('gx', 'gy', 'gz'))  81.5 us
    unnamed x203, local copies, waits for them, and re-layouts  17 us
    ppermute x6, waiting for transfers between devices, extended(): lax.ppermute(lax.slice_in_dim(block, block.shape[dim] - width, None, axis...  17 us
    ppermute x6, starting transfers between devices, extended(): lax.ppermute(lax.slice_in_dim(block, 0, width, axis=dim), axis, backward)  16.3 us
    ppermute x6, waiting for transfers between devices, extended(): lax.ppermute(lax.slice_in_dim(block, 0, width, axis=dim), axis, backward)  14.8 us
    reduce_sum x42, other arithmetic, apply_hessian(): summed = summed + jnp.sum(coupling[None] * neighbour[:, None], axis=2)  12.5 us
  transfers between devices with their start and end apart: 12, of which 8 were waited for; matrix products, arithmetic and copies ran while one was open for 6% of the time, Pallas kernels for 0%

commit v1 on v0

--- a/solution.py
+++ b/solution.py
@@ -111,7 +111,9 @@
     row_count = start_block[0].size * device_count
     blocks = offset_blocks(pair_blocks, slot_map)
     onsite = onsite_blocks(blocks)
-    start_gram = lax.psum(local_gram(start_block, start_block), ("gx", "gy", "gz")) / row_count
+    start_gram = (
+        lax.psum(lax.psum(local_gram(start_block, start_block), "gx"), ("gy", "gz")) / row_count
+    )
     lower0, inverse0 = inverse_factor(start_gram)
     basis1 = combine(inverse0, start_block)
     image1 = apply_hessian(basis1, blocks, onsite)

time: 524 us -> 640 us (1.22)
  blocking collectives: 377 us -> 464 us
  starting transfers between devices: 19.9 us -> 52 us
    psum x1 -> x2, blocking collectives: 81.5 us -> 168 us  [the longest x1 144 us: local(): lax.psum(lax.psum(local_gram(start_block, start_block), 'gx'), ('gy', 'gz'))]
    ppermute x6, starting transfers between devices: 3.56 us -> 43.7 us  [extended(): lax.ppermute(lax.slice_in_dim(block, block.shape[dim] - width, None, axis...]
    ppermute x6, starting transfers between devices: 16.3 us -> 8.29 us  [extended(): lax.ppermute(lax.slice_in_dim(block, 0, width, axis=dim), axis, backward)]
    ppermute x6, waiting for transfers between devices: 17 us -> 9.86 us  [extended(): lax.ppermute(lax.slice_in_dim(block, block.shape[dim] - width, None, axis...]
  transfers between devices with their start and end apart: 12 -> 12, of which waited for: 8 -> 8; matrix products, arithmetic and copies ran while one was open for 6% -> 5% of each run, Pallas kernels for 0% -> 0%
where the time goes in v1:
time: 640 us; the launch traced here: 639 us
  blocking collectives  464 us (72%)
  starting transfers between devices  52 us (8%)
  other arithmetic  45.5 us (7%)
  local copies, waits for them, and re-layouts  39 us (6%)
  waiting for transfers between devices  28.9 us (5%)
  matrix products  7.11 us (1%)
    psum x2, blocking collectives, lanczos_step(): alpha = lax.psum(local_gram(image, basis), ('gx', 'gy', 'gz')) / row_count  149 us
    psum x2, blocking collectives, lanczos_step(): lax.psum(local_gram(residual, residual), ('gx', 'gy', 'gz')) / row_count  147 us
    psum x1, blocking collectives, local(): lax.psum(lax.psum(local_gram(start_block, start_block), 'gx'), ('gy', 'gz'))  144 us
    ppermute x6, starting transfers between devices, extended(): lax.ppermute(lax.slice_in_dim(block, block.shape[dim] - width, None, axis...  43.7 us
    psum x1, blocking collectives, local(): lax.psum(local_gram(start_block, start_block), 'gx')  23.7 us
    ppermute x6, waiting for transfers between devices, extended(): lax.ppermute(lax.slice_in_dim(block, 0, width, axis=dim), axis, backward)  19 us
    unnamed x203, local copies, waits for them, and re-layouts  17 us
  transfers between devices with their start and end apart: 12, of which 8 were waited for; matrix products, arithmetic and copies ran while one was open for 5% of the time, Pallas kernels for 0%

profile of v1, /device:TPU:1, one launch (start us, length us, event | category | flops | bytes accessed | tf_op | source)
XLA Modules:
  0.0 638.7 jit_solution(18299998534936220854)
XLA Ops:
  0.6 1.2 reshape.1549
  1.8 1.6 convolution_bitcast_fusion.2
  3.4 23.7 %psum.42 = f32[32,32]{0,1:T(8,128)S(1)} all-reduce(f32[32,32]{0,1:T(8,128)S(1)} %convolution_bitcast_fusion.2), channel_id=1, replica_groups=mesh['gx'=8,'gy'=4,'gz'=8] {'gx'}, use_global_device_ids=true, to_apply=%region_1.2 | all-reduce | flops 1024 | bytes 8192 | tf_op jit(solution)/shard_map/psum | solution.py:115
  27.1 144.3 %psum.43 = f32[32,32]{0,1:T(8,128)S(1)} all-reduce(f32[32,32]{0,1:T(8,128)S(1)} %psum.42), channel_id=1, replica_groups=mesh['gx'=8,'gy'=4,'gz'=8] {'gy','gz'}, use_global_device_ids=true, to_apply=%region_2.3 | all-reduce | flops 1024 | bytes 8192 | tf_op jit(solution)/shard_map/psum | solution.py:115
  171.5 2.9 cholesky.59
  175.8 2.4 custom-call.7
  179.3 29.6 %collective-permute-start = (f32[32,3,2,1,4,128]{5,0,4,3,2,1:T(8,128)S(1)}, f32[32,3,2,1,4,128]{5,0,4,3,2,1:T(8,128)S(1)}, u32[]{:S(2)}, u32[]{:S(2)}) collective-permute-start(f32[32,3,2,1,4,128]{5,0,4,3,2,1:T(8,128)S(1)} %copy.391), channel_id=1, source_target_pairs={{0,32},{32,64},{64,96},{96,128},{128,160},{160,192},{192,224},{224... | collective-permute-start | bytes 1179656 | tf_op jit(solution)/shard_map/ppermute | solution.py:15
  208.8 1.9 collective-permute-start.1
  211.1 2.5 select_reduce_fusion.13
  222.7 4.8 collective-permute-start.2
  227.5 1.0 collective-permute-start.3
  231.7 1.0 collective-permute-done.2
  232.7 9.0 %collective-permute-done.3 = f32[32,3,2,3,1,128]{5,0,4,3,2,1:T(8,128)S(1)} collective-permute-done((f32[32,3,2,3,1,128]{5,0,4,3,2,1:T(8,128)S(1)}, f32[32,3,2,3,1,128]{5,0,4,3,2,1:T(8,128)S(1)}, u32[]{:S(2)}, u32[]{:S(2)}) %collective-permute-start.3) | collective-permute-done | bytes 294944 | tf_op jit(solution)/shard_map/ppermute | solution.py:18
  242.6 1.8 fusion.52
  244.5 2.8 copy.507
  247.9 1.3 copy.506
  249.2 4.7 collective-permute-start.4
  253.9 1.7 multiply_reduce_fusion.36
  255.6 2.7 copy.419
  259.2 1.5 copy.395
  260.8 1.4 fusion.8
  268.0 74.9 %psum.44 = f32[32,32]{0,1:T(8,128)S(1)} all-reduce(f32[32,32]{0,1:T(8,128)S(1)} %fusion.56), channel_id=1, replica_groups=mesh['gx'=8,'gy'=4,'gz'=8] {'gx','gy','gz'}, use_global_device_ids=true, to_apply=%region_48.51 | all-reduce | flops 1024 | bytes 8192 | tf_op jit(solution)/shard_map/psum | solution.py:101
  343.9 73.4 %psum.45 = f32[32,32]{0,1:T(8,128)S(1)} all-reduce(f32[32,32]{0,1:T(8,128)S(1)} %fusion.57), channel_id=1, replica_groups=mesh['gx'=8,'gy'=4,'gz'=8] {'gx','gy','gz'}, use_global_device_ids=true, to_apply=%region_49.52 | all-reduce | flops 1024 | bytes 8192 | tf_op jit(solution)/shard_map/psum | solution.py:105
  417.4 2.9 cholesky.70
  421.6 2.4 custom-call.8
  428.3 2.1 collective-permute-done.6
  430.6 2.7 collective-permute-done.7
  433.4 1.7 collective-permute-start.8
  435.0 1.6 collective-permute-start.9
  439.2 3.5 collective-permute-done.8
  442.7 7.3 %collective-permute-done.9 = f32[32,3,2,3,1,128]{5,0,4,3,2,1:T(8,128)S(1)} collective-permute-done((f32[32,3,2,3,1,128]{5,0,4,3,2,1:T(8,128)S(1)}, f32[32,3,2,3,1,128]{5,0,4,3,2,1:T(8,128)S(1)}, u32[]{:S(2)}, u32[]{:S(2)}) %collective-permute-start.9) | collective-permute-done | bytes 294944 | tf_op jit(solution)/shard_map/ppermute | solution.py:18
  451.0 1.8 fusion.51
  452.8 2.8 copy.509
  455.6 3.1 collective-permute-start.11
  458.7 1.5 multiply_reduce_fusion.6
  460.1 1.3 copy.508
  461.5 2.3 collective-permute-start.10
  463.8 1.5 copy.488
  465.3 2.2 maximum_bitcast_fusion.4
  468.4 2.4 collective-permute-done.10
  470.8 1.5 copy.486
  472.4 1.4 fusion.4
  479.5 74.4 %psum.46 = f32[32,32]{0,1:T(8,128)S(1)} all-reduce(f32[32,32]{0,1:T(8,128)S(1)} %fusion.59), channel_id=1, replica_groups=mesh['gx'=8,'gy'=4,'gz'=8] {'gx','gy','gz'}, use_global_device_ids=true, to_apply=%region_80.83 | all-reduce | flops 1024 | bytes 8192 | tf_op jit(solution)/shard_map/psum | solution.py:101
  555.7 73.3 %psum.47 = f32[32,32]{0,1:T(8,128)S(1)} all-reduce(f32[32,32]{0,1:T(8,128)S(1)} %fusion.60), channel_id=1, replica_groups=mesh['gx'=8,'gy'=4,'gz'=8] {'gx','gy','gz'}, use_global_device_ids=true, to_apply=%region_81.84 | all-reduce | flops 1024 | bytes 8192 | tf_op jit(solution)/shard_map/psum | solution.py:105
  629.0 2.9 cholesky.81
  632.6 1.3 select_bitcast_fusion
  633.9 2.4 custom-call.9
  637.0 1.0 copy.497
  (338 shorter events, 43.0 us)
Async XLA Ops:
  3.4 207.3 %copy-start.95 = (s32[16,2,1,4,128]{4,3,2,1,0:T(4,128)S(1)}, s32[16,2,1,4,128]{4,3,2,1,0:T(4,128)}, u32[]{:S(2)}) copy-start(s32[16,2,1,4,128]{4,3,2,1,0:T(4,128)} %param.8) | copy-start | bytes 196612
  175.1 35.9 %copy-start.35 = (f32[3,3,16,2,1,4,128]{6,5,4,3,2,1,0:T(4,128)S(1)}, f32[3,3,16,2,1,4,128]{6,5,4,3,2,1,0:T(4,128)}, u32[]{:S(2)}) copy-start(f32[3,3,16,2,1,4,128]{6,5,4,3,2,1,0:T(4,128)} %param.7) | copy-start | bytes 1769476
  179.3 43.2 %collective-permute-start = (f32[32,3,2,1,4,128]{5,0,4,3,2,1:T(8,128)S(1)}, f32[32,3,2,1,4,128]{5,0,4,3,2,1:T(8,128)S(1)}, u32[]{:S(2)}, u32[]{:S(2)}) collective-permute-start(f32[32,3,2,1,4,128]{5,0,4,3,2,1:T(8,128)S(1)} %copy.391), channel_id=1, source_target_pairs={{0,32},{32,64},{64,96},{96,128},{128,160},{160,192},{192,224},{224... | collective-permute-start | bytes 1179656 | tf_op jit(solution)/shard_map/ppermute | solution.py:15
  208.8 13.8 %collective-permute-start.1 = (f32[32,3,2,1,4,128]{5,0,4,3,2,1:T(8,128)S(1)}, f32[32,3,2,1,4,128]{5,0,4,3,2,1:T(8,128)S(1)}, u32[]{:S(2)}, u32[]{:S(2)}) collective-permute-start(f32[32,3,2,1,4,128]{5,0,4,3,2,1:T(8,128)S(1)} %copy.391), channel_id=1, source_target_pairs={{32,0},{64,32},{96,64},{128,96},{160,128},{192,160},{224,192},{0,2... | collective-permute-start | bytes 1179656 | tf_op jit(solution)/shard_map/ppermute | solution.py:18
  216.8 12.4 %copy-start.84 = (f32[3,3,4,128]{3,2,0,1:T(4,128)}, f32[3,3,4,128]{3,2,0,1:T(4,128)S(1)}, u32[]{:S(2)}) copy-start(f32[3,3,4,128]{3,2,0,1:T(4,128)S(1)} %get-tuple-element.159) | copy-start | bytes 55300
  216.8 13.1 %copy-start.82 = (f32[3,3,4,128]{3,2,0,1:T(4,128)}, f32[3,3,4,128]{3,2,0,1:T(4,128)S(1)}, u32[]{:S(2)}) copy-start(f32[3,3,4,128]{3,2,0,1:T(4,128)S(1)} %get-tuple-element.162) | copy-start | bytes 55300
  217.5 13.4 %copy-start.80 = (f32[3,3,4,128]{3,2,0,1:T(4,128)}, f32[3,3,4,128]{3,2,0,1:T(4,128)S(1)}, u32[]{:S(2)}) copy-start(f32[3,3,4,128]{3,2,0,1:T(4,128)S(1)} %get-tuple-element.194) | copy-start | bytes 55300
  219.4 10.6 %copy-start.88 = (f32[3,3,4,128]{3,2,0,1:T(4,128)}, f32[3,3,4,128]{3,2,0,1:T(4,128)S(1)}, u32[]{:S(2)}) copy-start(f32[3,3,4,128]{3,2,0,1:T(4,128)S(1)} %get-tuple-element.190) | copy-start | bytes 55300
  219.4 11.4 %copy-start.86 = (f32[3,3,4,128]{3,2,0,1:T(4,128)}, f32[3,3,4,128]{3,2,0,1:T(4,128)S(1)}, u32[]{:S(2)}) copy-start(f32[3,3,4,128]{3,2,0,1:T(4,128)S(1)} %get-tuple-element.189) | copy-start | bytes 55300
  220.7 1.8 copy-start.90
  220.7 1.8 copy-start.92
  220.8 1.9 copy-start.36
  222.7 10.0 %collective-permute-start.2 = (f32[32,3,2,3,1,128]{5,0,4,3,2,1:T(8,128)S(1)}, f32[32,3,2,3,1,128]{5,0,4,3,2,1:T(8,128)S(1)}, u32[]{:S(2)}, u32[]{:S(2)}) collective-permute-start(f32[32,3,2,3,1,128]{5,0,4,3,2,1:T(8,128)S(1)} %get-tuple-element.115), channel_id=1, source_target_pairs={{0,8},{8,16},{16,24},{24,0},{1,9},{9,17},{17,25},{25,1},{2,10},{10... | collective-permute-start | bytes 884744 | tf_op jit(solution)/shard_map/ppermute | solution.py:15
  227.5 14.2 %collective-permute-start.3 = (f32[32,3,2,3,1,128]{5,0,4,3,2,1:T(8,128)S(1)}, f32[32,3,2,3,1,128]{5,0,4,3,2,1:T(8,128)S(1)}, u32[]{:S(2)}, u32[]{:S(2)}) collective-permute-start(f32[32,3,2,3,1,128]{5,0,4,3,2,1:T(8,128)S(1)} %get-tuple-element.116), channel_id=1, source_target_pairs={{8,0},{16,8},{24,16},{0,24},{9,1},{17,9},{25,17},{1,25},{10,2},{18... | collective-permute-start | bytes 884744 | tf_op jit(solution)/shard_map/ppermute | solution.py:18
  232.7 9.0 %copy-start.8 = (f32[32,3,2,3,1,128]{5,0,4,3,2,1:T(8,128)}, f32[32,3,2,3,1,128]{5,0,4,3,2,1:T(8,128)S(1)}, u32[]{:S(2)}) copy-start(f32[32,3,2,3,1,128]{5,0,4,3,2,1:T(8,128)S(1)} %collective-permute-done.2) | copy-start | bytes 884740
  247.3 8.3 %collective-permute-start.5 = (f32[32,3,2,3,6,1]{0,2,5,4,3,1:T(2,128)}, f32[32,3,2,3,6,1]{0,2,5,4,3,1:T(2,128)}, u32[]{:S(2)}, u32[]{:S(2)}) collective-permute-start(f32[32,3,2,3,6,1]{0,2,5,4,3,1:T(2,128)} %copy.507), channel_id=1, source_target_pairs={{1,0},{2,1},{3,2},{4,3},{5,4},{6,5},{7,6},{0,7},{9,8},{10,9},{11,1... | collective-permute-start | bytes 41480 | tf_op jit(solution)/shard_map/ppermute | solution.py:18
  249.2 10.0 %collective-permute-start.4 = (f32[32,3,2,3,6,1]{0,2,5,4,3,1:T(2,128)}, f32[32,3,2,3,6,1]{0,2,5,4,3,1:T(2,128)}, u32[]{:S(2)}, u32[]{:S(2)}) collective-permute-start(f32[32,3,2,3,6,1]{0,2,5,4,3,1:T(2,128)} %copy.506), channel_id=1, source_target_pairs={{0,1},{1,2},{2,3},{3,4},{4,5},{5,6},{6,7},{7,0},{8,9},{9,10},{10,1... | collective-permute-start | bytes 41480 | tf_op jit(solution)/shard_map/ppermute | solution.py:15
  260.8 1.5 copy-start.72
  260.8 1.5 copy-start.9
  260.8 1.5 copy-start.11
  262.4 1.5 copy-start
  421.6 132.9 %copy-start.94 = (f32[32,32]{1,0:T(8,128)}, f32[32,32]{1,0:T(8,128)S(1)}, u32[]{:S(2)}) copy-start(f32[32,32]{1,0:T(8,128)S(1)} %get-tuple-element.76) | copy-start | bytes 12292
  424.3 1.6 copy-start.37
  424.3 1.6 copy-start.93
  424.8 2.0 copy-start.2
  424.8 2.0 copy-start.39
  424.8 2.0 copy-start.91
  425.1 5.3 collective-permute-start.6
  425.7 7.5 %collective-permute-start.7 = (f32[32,3,2,1,4,128]{5,0,4,3,2,1:T(8,128)S(1)}, f32[32,3,2,1,4,128]{5,0,4,3,2,1:T(8,128)S(1)}, u32[]{:S(2)}, u32[]{:S(2)}) collective-permute-start(f32[32,3,2,1,4,128]{5,0,4,3,2,1:T(8,128)S(1)} %copy.482), channel_id=1, source_target_pairs={{32,0},{64,32},{96,64},{128,96},{160,128},{192,160},{224,192},{0,2... | collective-permute-start | bytes 1179656 | tf_op jit(solution)/shard_map/ppermute | solution.py:18
  430.6 6.2 copy-start.85
  433.3 4.2 copy-start.83
  433.3 4.2 copy-start.89
  433.3 5.1 copy-start.81
  433.3 5.1 copy-start.87
  433.4 9.4 %collective-permute-start.8 = (f32[32,3,2,3,1,128]{5,0,4,3,2,1:T(8,128)S(1)}, f32[32,3,2,3,1,128]{5,0,4,3,2,1:T(8,128)S(1)}, u32[]{:S(2)}, u32[]{:S(2)}) collective-permute-start(f32[32,3,2,3,1,128]{5,0,4,3,2,1:T(8,128)S(1)} %get-tuple-element.113), channel_id=1, source_target_pairs={{0,8},{8,16},{16,24},{24,0},{1,9},{9,17},{17,25},{25,1},{2,10},{10... | collective-permute-start | bytes 884744 | tf_op jit(solution)/shard_map/ppermute | solution.py:15
  435.0 15.0 %collective-permute-start.9 = (f32[32,3,2,3,1,128]{5,0,4,3,2,1:T(8,128)S(1)}, f32[32,3,2,3,1,128]{5,0,4,3,2,1:T(8,128)S(1)}, u32[]{:S(2)}, u32[]{:S(2)}) collective-permute-start(f32[32,3,2,3,1,128]{5,0,4,3,2,1:T(8,128)S(1)} %get-tuple-element.114), channel_id=1, source_target_pairs={{8,0},{16,8},{24,16},{0,24},{9,1},{17,9},{25,17},{1,25},{10,2},{18... | collective-permute-start | bytes 884744 | tf_op jit(solution)/shard_map/ppermute | solution.py:18
  442.7 7.3 %copy-start.4 = (f32[32,3,2,3,1,128]{5,0,4,3,2,1:T(8,128)}, f32[32,3,2,3,1,128]{5,0,4,3,2,1:T(8,128)S(1)}, u32[]{:S(2)}) copy-start(f32[32,3,2,3,1,128]{5,0,4,3,2,1:T(8,128)S(1)} %collective-permute-done.8) | copy-start | bytes 884740
  455.6 8.1 %collective-permute-start.11 = (f32[32,3,2,3,6,1]{0,2,5,4,3,1:T(2,128)}, f32[32,3,2,3,6,1]{0,2,5,4,3,1:T(2,128)}, u32[]{:S(2)}, u32[]{:S(2)}) collective-permute-start(f32[32,3,2,3,6,1]{0,2,5,4,3,1:T(2,128)} %copy.509), channel_id=1, source_target_pairs={{1,0},{2,1},{3,2},{4,3},{5,4},{6,5},{7,6},{0,7},{9,8},{10,9},{11,1... | collective-permute-start | bytes 41480 | tf_op jit(solution)/shard_map/ppermute | solution.py:18
  461.5 9.3 %collective-permute-start.10 = (f32[32,3,2,3,6,1]{0,2,5,4,3,1:T(2,128)}, f32[32,3,2,3,6,1]{0,2,5,4,3,1:T(2,128)}, u32[]{:S(2)}, u32[]{:S(2)}) collective-permute-start(f32[32,3,2,3,6,1]{0,2,5,4,3,1:T(2,128)} %copy.508), channel_id=1, source_target_pairs={{0,1},{1,2},{2,3},{3,4},{4,5},{5,6},{6,7},{7,0},{8,9},{9,10},{10,1... | collective-permute-start | bytes 41480 | tf_op jit(solution)/shard_map/ppermute | solution.py:15
  465.3 2.2 copy-start.1
  465.3 2.2 copy-start.59
  465.3 2.2 copy-start.63
  472.3 1.4 copy-start.65
  472.3 1.5 copy-start.79
  472.3 1.6 copy-start.55
  472.3 1.6 copy-start.73
  472.3 1.7 copy-start.57
  472.4 1.7 copy-start.77
  (60 other events, 58.4 us)
